TPU v7x, 32 devices: a whole 2x2x4 slice. The times are simulated.
32 devices in a mesh: clips: 2 (over y), row: 4 (over x, core), col: 4 (over z).
Axes of the slice: x: 2, y: 2, z: 4, core: 2. Of those that a mesh axis runs over, the one named last changes fastest.
Arguments:
- clip_tokens: bfloat16 [2048, 6144], P(('clips', 'col'), 'row'), parts along dimension 0, may hold values from -12 to 12
- modulation: float32 [8, 6, 6144], P('clips', None, 'row'), parts along dimension 0, may hold values from -3 to 3
- w_qkv: bfloat16 [6144, 3, 4096], P('row', None, 'col'), may hold values from -3 to 3
- w_out: bfloat16 [4096, 6144], P('col', 'row'), may hold values from -0.09375 to 0.09375
- w_up: bfloat16 [6144, 12288], P('row', 'col'), may hold values from -0.078125 to 0.078125
- up_bias: float32 [12288], P('col'), may hold values from -3 to 3
- w_down: bfloat16 [12288, 6144], P('col', 'row'), may hold values from -0.0546875 to 0.0546875
- guide_num: int32 [8], P('clips'), parts along dimension 0, may hold values from -3 to 10, as said below
Outputs:
- guided: bfloat16 [512, 6144], P(('clips', 'col'), 'row'), parts along dimension 0
There are 2 independent parts, one for each index of `clips`. A program takes and returns all parts, laid end to end along the dimension named above; an argument that names none is the same for every part. Nothing has to cross between parts.
Inputs may be any that keep to these rules, and one draw needn't show every extreme that they name: `guide_num`: the three negative numerators are -1, -2 and -3 in some order, and the positive one makes the four sum to 4.
All inputs are finite; a program needn't handle non-finite values.
Results may differ from a plain program's by a relative error of at most 0.019.
Values may be sent and summed in bfloat16 or wider, within the bound.
A program may use at most 128 MiB of HBM per device.

v0:
```python
import jax
import jax.numpy as jnp
from jax import lax
from jax.sharding import PartitionSpec as P

D = 6144
HEAD_DIM = 128
eps = 1e-06


def normalize(values, shift, scale):
    totals = lax.psum((jnp.sum(values, axis=1), jnp.sum(values * values, axis=1)), "row")
    mean = totals[0] / D
    variance = totals[1] / D - mean * mean
    normed = (values - mean[:, None]) * lax.rsqrt(variance + eps)[:, None]
    branches = shift.shape[0]
    shaped = normed.reshape(-1, branches, values.shape[1]) * (1.0 + scale[None]) + shift[None]
    return shaped.reshape(values.shape)


def general_layer(clip_tokens, modulation, w_qkv, w_out, w_up, up_bias, w_down, guide_num):
    branches = modulation.shape[0]
    feat_rows = w_qkv.shape[0]
    head_cols = w_qkv.shape[2]
    heads_here = head_cols // HEAD_DIM
    x_rows = clip_tokens.astype(jnp.float32)
    first = normalize(x_rows, modulation[:, 0], modulation[:, 1]).astype(jnp.bfloat16)
    w_flat = w_qkv.reshape(feat_rows, 3 * head_cols)
    partial_qkv = jnp.dot(
        lax.all_gather(first, "col", axis=0, tiled=True), w_flat, preferred_element_type=jnp.float32
    )
    scale_score = 1.0 / jnp.sqrt(jnp.float32(HEAD_DIM))
    qkv = lax.psum_scatter(partial_qkv.astype(jnp.bfloat16), "row", scatter_dimension=0, tiled=True)
    query3 = qkv[:, :head_cols].reshape(-1, heads_here, HEAD_DIM)
    query_rows = query3.shape[0]
    piece = (
        lax.all_gather(qkv[:, head_cols : 2 * head_cols], "row", axis=0, tiled=True),
        lax.all_gather(qkv[:, 2 * head_cols :], "row", axis=0, tiled=True),
    )
    top = jnp.full((heads_here, query_rows), -1e30, jnp.float32)
    rows = piece[0].shape[0]
    key_heads = piece[0].reshape(rows, heads_here, HEAD_DIM)
    value_heads = piece[1].reshape(rows, heads_here, HEAD_DIM)
    scores = (
        jnp.einsum("qhd,khd->hqk", query3, key_heads, preferred_element_type=jnp.float32)
        * scale_score
    )
    query_branch = jnp.arange(query3.shape[0], dtype=jnp.int32) % branches
    key_branch = jnp.arange(rows, dtype=jnp.int32) % branches
    allowed = (query_branch[:, None] == key_branch[None, :])[None]
    masked = jnp.where(allowed, scores, -1e30)
    new_top = jnp.maximum(top, jnp.max(masked, axis=-1))
    weights = jnp.where(allowed, jnp.exp(masked - new_top[..., None]), 0.0)
    denom = jnp.sum(weights, axis=-1)
    accum = jnp.einsum(
        "hqk,khd->hqd",
        weights.astype(jnp.bfloat16),
        value_heads,
        preferred_element_type=jnp.float32,
    )
    att = (accum / denom[..., None]).transpose(1, 0, 2).reshape(-1, head_cols).astype(jnp.bfloat16)
    partial_out = jnp.dot(
        lax.all_gather(att, "row", axis=0, tiled=True), w_out, preferred_element_type=jnp.float32
    )
    out_rows = lax.psum_scatter(
        partial_out.astype(jnp.bfloat16), "col", scatter_dimension=0, tiled=True
    ).astype(jnp.float32)
    by_branch = x_rows.shape[0] // branches
    resid = (
        x_rows.reshape(by_branch, branches, feat_rows)
        + modulation[None, :, 2] * out_rows.reshape(by_branch, branches, feat_rows)
    ).reshape(x_rows.shape)
    second = normalize(resid, modulation[:, 3], modulation[:, 4]).astype(jnp.bfloat16)
    partial_up = jnp.dot(
        lax.all_gather(second, "col", axis=0, tiled=True), w_up, preferred_element_type=jnp.float32
    )
    up_rows = lax.psum_scatter(
        partial_up.astype(jnp.bfloat16), "row", scatter_dimension=0, tiled=True
    ).astype(jnp.float32)
    act = jax.nn.gelu(up_rows + up_bias[None], approximate=True).astype(jnp.bfloat16)
    partial_down = jnp.dot(
        lax.all_gather(act, "row", axis=0, tiled=True), w_down, preferred_element_type=jnp.float32
    )
    guide_weights = guide_num.astype(jnp.float32) / 4.0
    weights_gate = guide_weights[:, None] * modulation[:, 5]
    combined = jnp.sum(partial_down.reshape(-1, branches, feat_rows) * weights_gate[None], axis=1)
    mlp_rows = lax.psum_scatter(
        combined.astype(jnp.bfloat16), "col", scatter_dimension=0, tiled=True
    ).astype(jnp.float32)
    resid_mix = jnp.sum(
        resid.reshape(by_branch, branches, feat_rows) * guide_weights[None, :, None], axis=1
    )
    return (resid_mix + mlp_rows).astype(jnp.bfloat16)


BF = jnp.bfloat16


def swap_row(value, distance):
    size = lax.axis_size("row")
    return lax.ppermute(value, "row", [(r, r ^ distance) for r in range(size)])


def sum_over_row(value):
    value = value + swap_row(value, 1)
    return value + swap_row(value, 2)


def scatter_row(partial, axis):
    me = lax.axis_index("row")
    half, core = (me // 2, me % 2)
    span = partial.shape[axis] // 4

    def piece(index):
        return lax.dynamic_slice_in_dim(partial, index * span, span, axis)

    far = swap_row(piece((1 - half) * 2 + 1 - core), 1)
    near = swap_row(piece(half * 2 + 1 - core), 1)
    away = piece((1 - half) * 2 + core).astype(jnp.float32) + far.astype(jnp.float32)
    came = swap_row(away.astype(BF), 2)
    kept = piece(half * 2 + core).astype(jnp.float32) + near.astype(jnp.float32)
    return kept + came.astype(jnp.float32)


def shift_col(value, distance):
    size = lax.axis_size("col")
    return lax.ppermute(value, "col", [(c, (c + distance) % size) for c in range(size)])


def gather_col(value):
    size = lax.axis_size("col")
    return jnp.stack([value] + [shift_col(value, k) for k in range(1, size)])


def in_order(blocks):
    size, me = (blocks.shape[0], lax.axis_index("col"))
    return jnp.stack(
        [lax.dynamic_index_in_dim(blocks, (me - k) % size, 0, False) for k in range(size)]
    )


def gather_row(value, other, axis):
    me = lax.axis_index("row")
    half, core = (me // 2, me % 2)
    beside = swap_row(value, 1)
    across = swap_row(other, 1)

    def pick(x, c):
        same = jnp.where(core == c, value, beside)
        away = jnp.where(core == c, other, across)
        return jnp.where(half == x, same, away)

    return jnp.concatenate([pick(0, 0), pick(0, 1), pick(1, 0), pick(1, 1)], axis=axis)


def apply_norm(values, totals, shift, scale):
    totals = totals.reshape(2, *values.shape[:3])
    mean = totals[0] / D
    variance = totals[1] / D - mean * mean
    normed = (values - mean[..., None]) * lax.rsqrt(variance + eps)[..., None]
    return (normed * (1.0 + scale[None, :, None]) + shift[None, :, None]).astype(BF)


def moments(values):
    return jnp.stack([jnp.sum(values, axis=-1), jnp.sum(values * values, axis=-1)]).reshape(2, -1)


def attend(q, k, v):
    scores = jnp.einsum("bhqd,bhkd->bhqk", q, k, preferred_element_type=jnp.float32)
    scores = scores / jnp.sqrt(jnp.float32(HEAD_DIM))
    weights = jnp.exp(scores - jnp.max(scores, axis=-1, keepdims=True))
    denom = jnp.sum(weights, axis=-1)
    mixed = jnp.einsum("bhqk,bhkd->bhqd", weights.astype(BF), v, preferred_element_type=jnp.float32)
    return (mixed / denom[..., None]).astype(BF)


GROUPS = 2


def head_layer(clip_tokens, modulation, w_qkv, w_out, w_up, up_bias, w_down, guide_num):
    branches = modulation.shape[0]
    feat_rows, _, head_cols = w_qkv.shape
    mine = head_cols // 4
    heads = mine // HEAD_DIM
    here = clip_tokens.shape[0] // branches
    wide = branches // GROUPS
    cols = lax.axis_size("col")
    w_flat = w_qkv.reshape(feat_rows, 3, 4, mine).transpose(0, 2, 1, 3).reshape(feat_rows, -1)
    by_branch = clip_tokens.reshape(here, branches, feat_rows).transpose(1, 0, 2)
    guide = guide_num.astype(jnp.float32) / 4.0
    gate = guide[:, None] * modulation[:, 5]
    parts = [slice(g * wide, (g + 1) * wide) for g in range(GROUPS)]
    tokens = cols * wide * here
    x_parts = [by_branch[p].reshape(wide * here, feat_rows) for p in parts]
    gathered = [lax.all_gather(x, "col", axis=0, tiled=True) for x in x_parts]
    gathered[0], w_flat = lax.optimization_barrier((gathered[0], w_flat))

    def project(g):
        mod = modulation[parts[g]]
        x_all = gathered[g].astype(jnp.float32).reshape(cols, wide, here, feat_rows)
        first = apply_norm(x_all, sum_over_row(moments(x_all)), mod[:, 0], mod[:, 1])
        first = first.reshape(tokens, feat_rows)
        partial = jnp.dot(first, w_flat, preferred_element_type=jnp.float32).astype(BF)
        return scatter_row(partial, 1).astype(BF)

    def attention(g, qkv):
        shaped = qkv.reshape(cols, wide, here, 3, heads, HEAD_DIM).transpose(3, 1, 4, 0, 2, 5)
        shaped = shaped.reshape(3, wide, heads, cols * here, HEAD_DIM)
        att = attend(shaped[0], shaped[1], shaped[2])
        att = att.reshape(wide, heads, cols, here, HEAD_DIM).transpose(2, 0, 3, 1, 4)
        att = att.reshape(tokens, mine)
        att_all = gather_row(att, swap_row(att, 2), 1)
        partial = jnp.dot(att_all, w_out, preferred_element_type=jnp.float32).astype(BF)
        return lax.psum_scatter(partial, "col", scatter_dimension=0, tiled=True)

    def residual(g, out):
        mod = modulation[parts[g]]
        x = x_parts[g].astype(jnp.float32).reshape(1, wide, here, feat_rows)
        out = out.astype(jnp.float32).reshape(1, wide, here, feat_rows)
        resid = x + mod[None, :, 2, None] * out
        second = apply_norm(resid, sum_over_row(moments(resid)), mod[:, 3], mod[:, 4])
        second = second.reshape(wide * here, feat_rows)
        mixed = jnp.sum(resid[0] * guide[parts[g]][:, None, None], axis=0)
        if g:
            seconds[-1], second = lax.optimization_barrier((seconds[-1], second))
        if g < GROUPS - 1:
            return (mixed, gather_col(second).reshape(tokens, feat_rows))
        return (mixed, lax.all_gather(second, "col", axis=0, tiled=True))

    def expand(g, second_all):
        partial = jnp.dot(second_all, w_up, preferred_element_type=jnp.float32).astype(BF)
        if g:
            before = acts[g - 1]
            partial, other = lax.optimization_barrier((partial, before[1]))
            acts[g - 1] = (before[0], other)
        up = scatter_row(partial, 0)
        act = jax.nn.gelu(up + up_bias[None], approximate=True).astype(BF)
        return (act, swap_row(act, 2))

    def contract(g, act):
        down = jnp.dot(gather_row(act[0], act[1], 0), w_down, preferred_element_type=jnp.float32)
        down = down.reshape(cols, wide, here, feat_rows)
        down = sum((down[:, b] * gate[parts[g]][b] for b in range(wide)))
        return in_order(down) if g < GROUPS - 1 else down

    every = range(GROUPS)
    qkv, acts = ([], [])
    for g in every:
        if g:
            gathered[g], qkv[-1] = lax.optimization_barrier((gathered[g], qkv[-1]))
        qkv.append(project(g))
    outs = [attention(g, qkv[g]) for g in every]
    mixed, seconds = ([], [])
    for g in every:
        out = outs[g]
        if g:
            out, seconds[-1] = lax.optimization_barrier((out, seconds[-1]))
        kept, second = residual(g, out)
        mixed.append(kept)
        seconds.append(second)
    for g in every:
        second = seconds[g]
        if g:
            second, act = lax.optimization_barrier((second, acts[-1][0]))
            acts[-1] = (act, acts[-1][1])
        acts.append(expand(g, second))
    total = sum((contract(g, acts[g]) for g in every))
    total = total.astype(BF).reshape(cols * here, feat_rows)
    mlp = lax.psum_scatter(total, "col", scatter_dimension=0, tiled=True)
    return (sum(mixed) + mlp.astype(jnp.float32)).astype(BF)


def on_device(*args):
    heads_here = args[2].shape[2] // HEAD_DIM
    if lax.axis_size("row") == 4 and heads_here % 4 == 0:
        return head_layer(*args)
    return general_layer(*args)


def solution(mesh):
    in_specs = (
        P(("clips", "col"), "row"),
        P("clips", None, "row"),
        P("row", None, "col"),
        P("col", "row"),
        P("row", "col"),
        P("col"),
        P("col", "row"),
        P("clips"),
    )
    out_specs = P(("clips", "col"), "row")
    return jax.shard_map(
        on_device, mesh=mesh, in_specs=in_specs, out_specs=out_specs, check_vma=False
    )
```

profile of v0, /device:TPU:0, one launch (start us, length us, event | category | flops | bytes accessed | tf_op | source)
XLA Modules:
  0.0 391.4 jit_solution(15030035954881024947)
XLA Ops:
  6.5 2.5 reshape.357
  12.3 12.6 %copy.32 = bf16[1536,3,1024]{0,2,1:T(8,128)(2,1)} copy(bf16[1536,3,1024]{2,0,1:T(8,128)(2,1)} %param.10) | data formatting | bytes 18874368 | tf_op args[2]
  24.9 8.0 %copy.33 = bf16[1536,4,3,256]{0,3,2,1:T(8,128)(2,1)} copy(bf16[1536,4,3,256]{0,3,1,2:T(8,128)(2,1)} %bitcast.146) | data formatting | bytes 18874368 | tf_op jit(solution)/shard_map/transpose | solution.py:188
  32.9 19.3 %all-gather.6.cloned.1.call-done = bf16[512,1536]{1,0:T(8,128)(2,1)} async-done(((bf16[128,1536]{1,0:T(8,128)(2,1)}), bf16[512,1536]{1,0:T(8,128)(2,1)}) %all-gather.6.cloned.1.call-update) | async-done | bytes 1572880 | tf_op jit(solution)/shard_map/all_gather | solution.py:195
  59.1 2.7 fusion.4
  61.8 9.6 %convolution_convert_fusion.3 = bf16[512,3072]{1,0:T(8,128)(2,1)S(1)} fusion(bf16[512,1536]{1,0:T(8,128)(2,1)S(1)} %fusion.4, bf16[1536,3072]{0,1:T(8,128)(2,1)} %bitcast.152), kind=kOutput, calls=%fused_computation.9 | convolution fusion | flops 4833411072 | bytes 14155776 | tf_op jit(solution)/shard_map/dot_general | solution.py:203
  76.2 2.5 add_convert_fusion.5
  80.2 18.4 %collective-permute-done.4 = bf16[512,768]{1,0:T(8,128)(2,1)} collective-permute-done((bf16[512,768]{1,0:T(8,128)(2,1)}, bf16[512,768]{1,0:T(8,128)(2,1)}, u32[]{:S(2)}, u32[]{:S(2)}) %collective-permute-start.4) | collective-permute-done | bytes 786464 | tf_op jit(solution)/shard_map/ppermute | solution.py:101
  98.6 2.8 add_convert_fusion.4
  101.4 2.7 reshape.362
  112.8 9.1 %convolution_convert_fusion.2 = bf16[512,3072]{1,0:T(8,128)(2,1)S(1)} fusion(bf16[512,1536]{1,0:T(8,128)(2,1)S(1)} %fusion.9, bf16[1536,3072]{0,1:T(8,128)(2,1)} %bitcast.153), kind=kOutput, calls=%fused_computation.8 | convolution fusion | flops 4833411072 | bytes 14155776 | tf_op jit(solution)/shard_map/dot_general | solution.py:203
  128.7 2.4 add_convert_fusion.3
  132.6 3.0 convolution_convert_fusion.5
  135.6 15.4 %collective-permute-done.12 = bf16[512,768]{1,0:T(8,128)(2,1)} collective-permute-done((bf16[512,768]{1,0:T(8,128)(2,1)}, bf16[512,768]{1,0:T(8,128)(2,1)}, u32[]{:S(2)}, u32[]{:S(2)}) %collective-permute-start.12) | collective-permute-done | bytes 786464 | tf_op jit(solution)/shard_map/ppermute | solution.py:101
  151.0 2.8 add_convert_fusion.2
  153.8 2.9 reshape.367
  161.3 6.1 %collective-permute-done.14 = bf16[512,256]{1,0:T(8,128)(2,1)S(1)} collective-permute-done((bf16[512,256]{1,0:T(8,128)(2,1)S(1)}, bf16[512,256]{1,0:T(8,128)(2,1)S(1)}, u32[]{:S(2)}, u32[]{:S(2)}) %collective-permute-start.14) | collective-permute-done | bytes 262176 | tf_op jit(solution)/shard_map/ppermute | solution.py:101
  169.0 3.0 convolution_convert_fusion.4
  183.1 2.2 collective-permute-start.20
  185.3 17.9 %collective-permute-done.18 = bf16[128,1536]{1,0:T(8,128)(2,1)S(1)} collective-permute-done((bf16[128,1536]{1,0:T(8,128)(2,1)S(1)}, bf16[128,1536]{1,0:T(8,128)(2,1)S(1)}, u32[]{:S(2)}, u32[]{:S(2)}) %collective-permute-start.18) | collective-permute-done | bytes 393248 | tf_op jit(solution)/shard_map/ppermute | solution.py:127
  203.3 26.2 %collective-permute-done.19 = bf16[128,1536]{1,0:T(8,128)(2,1)S(1)} collective-permute-done((bf16[128,1536]{1,0:T(8,128)(2,1)S(1)}, bf16[128,1536]{1,0:T(8,128)(2,1)S(1)}, u32[]{:S(2)}, u32[]{:S(2)}) %collective-permute-start.19) | collective-permute-done | bytes 393248 | tf_op jit(solution)/shard_map/ppermute | solution.py:127
  240.2 8.1 %convolution_convert_fusion.1 = bf16[512,3072]{1,0:T(8,128)(2,1)S(1)} fusion(bf16[512,1536]{1,0:T(8,128)(2,1)} %bitcast.162, bf16[1536,3072]{1,0:T(8,128)(2,1)} %param.12), kind=kOutput, calls=%fused_computation.7 | convolution fusion | flops 4833411072 | bytes 14155776 | tf_op jit(solution)/shard_map/dot_general | solution.py:231
  252.2 2.2 add_convert_fusion.1
  255.9 18.4 %collective-permute-done.25 = bf16[128,3072]{1,0:T(8,128)(2,1)} collective-permute-done((bf16[128,3072]{1,0:T(8,128)(2,1)}, bf16[128,3072]{1,0:T(8,128)(2,1)}, u32[]{:S(2)}, u32[]{:S(2)}) %collective-permute-start.25) | collective-permute-done | bytes 786464 | tf_op jit(solution)/shard_map/ppermute | solution.py:101
  274.3 3.1 fusion.33
  278.8 16.8 %all-gather.8.cloned.1.call-done = bf16[512,1536]{1,0:T(8,128)(2,1)} async-done(((bf16[128,1536]{1,0:T(8,128)(2,1)}), bf16[512,1536]{1,0:T(8,128)(2,1)}) %all-gather.8.cloned.1.call-update) | async-done | bytes 1572880 | tf_op jit(solution)/shard_map/all_gather | solution.py:228
  295.7 8.3 %convolution_convert_fusion = bf16[512,3072]{1,0:T(8,128)(2,1)S(1)} fusion(bf16[512,1536]{1,0:T(8,128)(2,1)} %all-gather.8.cloned.1.call-done, bf16[1536,3072]{1,0:T(8,128)(2,1)} %param.12), kind=kOutput, calls=%fused_computation.6 | convolution fusion | flops 4833411072 | bytes 14155776 | tf_op jit(solution)/shard_map/dot_general | solution.py:231
  312.6 16.3 %collective-permute-done.31 = bf16[128,3072]{1,0:T(8,128)(2,1)S(1)} collective-permute-done((bf16[128,3072]{1,0:T(8,128)(2,1)S(1)}, bf16[128,3072]{1,0:T(8,128)(2,1)S(1)}, u32[]{:S(2)}, u32[]{:S(2)}) %collective-permute-start.31) | collective-permute-done | bytes 786464 | tf_op jit(solution)/shard_map/ppermute | solution.py:101
  331.2 8.9 %fusion.10 = f32[512,1536]{1,0:T(8,128)S(1)} fusion(bf16[3072,1536]{1,0:T(8,128)(2,1)} %param.14, bf16[128,3072]{1,0:T(8,128)(2,1)S(1)} %get-tuple-element.48, bf16[128,3072]{1,0:T(8,128)(2,1)S(1)} %get-tuple-element.49, bf16[128,3072]{1,0:T(8,128)(2,1)S(1)} %get-tuple-element.50, bf16[128,3072]{1,0:T(8,128)(2,1)S(1)} %get-tuple-element.47), kind=kOutput, calls=%fused_computation.20 | convolution fusion | flops 4844421120 | bytes 15728640 | tf_op jit(solution)/shard_map/dot_general | solution.py:241
  340.1 8.3 %collective-permute-done.33 = bf16[128,3072]{1,0:T(8,128)(2,1)S(1)} collective-permute-done((bf16[128,3072]{1,0:T(8,128)(2,1)S(1)}, bf16[128,3072]{1,0:T(8,128)(2,1)S(1)}, u32[]{:S(2)}, u32[]{:S(2)}) %collective-permute-start.33) | collective-permute-done | bytes 786464 | tf_op jit(solution)/shard_map/ppermute | solution.py:101
  351.1 5.0 %fusion.18 = f32[512,1536]{1,0:T(8,128)S(1)} fusion(bf16[3072,1536]{1,0:T(8,128)(2,1)S(1)} %bitcast.204, bf16[128,3072]{1,0:T(8,128)(2,1)S(1)} %get-tuple-element.54, bf16[128,3072]{1,0:T(8,128)(2,1)S(1)} %get-tuple-element.55, bf16[128,3072]{1,0:T(8,128)(2,1)S(1)} %get-tuple-element.56, bf16[128,3072]{1,0:T(8,128)(2,1)S(1)} %get-tuple-element.53), kind=kOutput, calls=%fused_computation.28 | convolution fusion | flops 4844421120 | bytes 15728640 | tf_op jit(solution)/shard_map/dot_general | solution.py:241
  357.8 24.6 %reduce-scatter.8.cloned.1.call-done = bf16[64,1536]{1,0:T(8,128)(2,1)} async-done(((bf16[256,1536]{1,0:T(8,128)(2,1)}), bf16[64,1536]{1,0:T(8,128)(2,1)}) %reduce-scatter.8.cloned.1.call-update) | async-done | bytes 196624 | tf_op jit(solution)/shard_map/reduce_scatter | solution.py:269
  (190 shorter events, 85.1 us)
Async XLA Ops:
  6.5 45.6 %all-gather.6.cloned.1.call-start = ((), (), s32[]{:S(2)}) async-start(), calls=%async_computation.4 | async-start | bytes 1966080 | tf_op jit(solution)/shard_map/all_gather | solution.py:195
  12.2 89.2 %all-gather.4.cloned.1.call-start = ((), (), s32[]{:S(2)}) async-start(), calls=%async_computation.3 | async-start | bytes 1966080 | tf_op jit(solution)/shard_map/all_gather | solution.py:195
  54.3 118.4 %reduce-scatter.4.cloned.1.call-start = ((), (), s32[]{:S(2)}) async-start(), calls=%async_computation.5 | async-start | bytes 1966080 | tf_op jit(solution)/shard_map/reduce_scatter | solution.py:214
  55.4 3.7 collective-permute-start.1
  73.6 6.6 %collective-permute-start.2 = (bf16[512,768]{1,0:T(8,128)(2,1)}, bf16[512,768]{1,0:T(8,128)(2,1)}, u32[]{:S(2)}, u32[]{:S(2)}) collective-permute-start(bf16[512,768]{1,0:T(8,128)(2,1)} %get-tuple-element.63), channel_id=1, source_target_pairs={{0,4},{4,0},{8,12},{12,8},{1,5},{5,1},{9,13},{13,9},{2,6},{6,2},{1... | collective-permute-start | bytes 2359304 | tf_op jit(solution)/shard_map/ppermute | solution.py:101
  78.7 19.9 %collective-permute-start.4 = (bf16[512,768]{1,0:T(8,128)(2,1)}, bf16[512,768]{1,0:T(8,128)(2,1)}, u32[]{:S(2)}, u32[]{:S(2)}) collective-permute-start(bf16[512,768]{1,0:T(8,128)(2,1)} %add_convert_fusion.5), channel_id=1, source_target_pairs={{0,8},{4,12},{8,0},{12,4},{1,9},{5,13},{9,1},{13,5},{2,10},{6,14},... | collective-permute-start | bytes 2359304 | tf_op jit(solution)/shard_map/ppermute | solution.py:101
  107.9 3.7 collective-permute-start.9
  110.8 13.8 %collective-permute-start.6 = (bf16[512,256]{1,0:T(8,128)(2,1)}, bf16[512,256]{1,0:T(8,128)(2,1)}, u32[]{:S(2)}, u32[]{:S(2)}) collective-permute-start(bf16[512,256]{1,0:T(8,128)(2,1)} %bitcast.145), channel_id=1, source_target_pairs={{0,8},{4,12},{8,0},{12,4},{1,9},{5,13},{9,1},{13,5},{2,10},{6,14},... | collective-permute-start | bytes 786440 | tf_op jit(solution)/shard_map/ppermute | solution.py:101
  124.1 4.6 %collective-permute-start.11 = (bf16[512,768]{1,0:T(8,128)(2,1)}, bf16[512,768]{1,0:T(8,128)(2,1)}, u32[]{:S(2)}, u32[]{:S(2)}) collective-permute-start(bf16[512,768]{1,0:T(8,128)(2,1)} %get-tuple-element.62), channel_id=1, source_target_pairs={{0,4},{4,0},{8,12},{12,8},{1,5},{5,1},{9,13},{13,9},{2,6},{6,2},{1... | collective-permute-start | bytes 2359304 | tf_op jit(solution)/shard_map/ppermute | solution.py:101
  124.1 3.0 collective-permute-start.5
  124.6 2.9 collective-permute-start.7
  124.6 11.0 %collective-permute-start.10 = (bf16[512,768]{1,0:T(8,128)(2,1)}, bf16[512,768]{1,0:T(8,128)(2,1)}, u32[]{:S(2)}, u32[]{:S(2)}) collective-permute-start(bf16[512,768]{1,0:T(8,128)(2,1)} %get-tuple-element.61), channel_id=1, source_target_pairs={{0,4},{4,0},{8,12},{12,8},{1,5},{5,1},{9,13},{13,9},{2,6},{6,2},{1... | collective-permute-start | bytes 2359304 | tf_op jit(solution)/shard_map/ppermute | solution.py:101
  131.1 19.9 %collective-permute-start.12 = (bf16[512,768]{1,0:T(8,128)(2,1)}, bf16[512,768]{1,0:T(8,128)(2,1)}, u32[]{:S(2)}, u32[]{:S(2)}) collective-permute-start(bf16[512,768]{1,0:T(8,128)(2,1)} %add_convert_fusion.3), channel_id=1, source_target_pairs={{0,8},{4,12},{8,0},{12,4},{1,9},{5,13},{9,1},{13,5},{2,10},{6,14},... | collective-permute-start | bytes 2359304 | tf_op jit(solution)/shard_map/ppermute | solution.py:101
  135.5 95.2 %reduce-scatter.6.cloned.1.call-start = ((), (), s32[]{:S(2)}) async-start(), calls=%async_computation.6 | async-start | bytes 1966080 | tf_op jit(solution)/shard_map/reduce_scatter | solution.py:214
  159.8 7.6 %collective-permute-start.14 = (bf16[512,256]{1,0:T(8,128)(2,1)S(1)}, bf16[512,256]{1,0:T(8,128)(2,1)S(1)}, u32[]{:S(2)}, u32[]{:S(2)}) collective-permute-start(bf16[512,256]{1,0:T(8,128)(2,1)S(1)} %bitcast.179), channel_id=1, source_target_pairs={{0,8},{4,12},{8,0},{12,4},{1,9},{5,13},{9,1},{13,5},{2,10},{6,14},... | collective-permute-start | bytes 786440 | tf_op jit(solution)/shard_map/ppermute | solution.py:101
  161.3 6.1 %collective-permute-start.13 = (bf16[512,256]{1,0:T(8,128)(2,1)S(1)}, bf16[512,256]{1,0:T(8,128)(2,1)S(1)}, u32[]{:S(2)}, u32[]{:S(2)}) collective-permute-start(bf16[512,256]{1,0:T(8,128)(2,1)S(1)} %bitcast.180), channel_id=1, source_target_pairs={{0,4},{4,0},{8,12},{12,8},{1,5},{5,1},{9,13},{13,9},{2,6},{6,2},{1... | collective-permute-start | bytes 786440 | tf_op jit(solution)/shard_map/ppermute | solution.py:101
  172.0 123.6 %all-gather.8.cloned.1.call-start = ((), (), s32[]{:S(2)}) async-start(), calls=%async_computation.7 | async-start | bytes 1966080 | tf_op jit(solution)/shard_map/all_gather | solution.py:228
  175.9 3.7 collective-permute-start.17
  181.0 22.2 %collective-permute-start.18 = (bf16[128,1536]{1,0:T(8,128)(2,1)S(1)}, bf16[128,1536]{1,0:T(8,128)(2,1)S(1)}, u32[]{:S(2)}, u32[]{:S(2)}) collective-permute-start(bf16[128,1536]{1,0:T(8,128)(2,1)S(1)} %bitcast.163), channel_id=1, source_target_pairs={{0,1},{1,2},{2,3},{3,0},{4,5},{5,6},{6,7},{7,4},{8,9},{9,10},{10,1... | collective-permute-start | bytes 1179656 | tf_op jit(solution)/shard_map/ppermute | solution.py:127
  181.6 47.8 %collective-permute-start.19 = (bf16[128,1536]{1,0:T(8,128)(2,1)S(1)}, bf16[128,1536]{1,0:T(8,128)(2,1)S(1)}, u32[]{:S(2)}, u32[]{:S(2)}) collective-permute-start(bf16[128,1536]{1,0:T(8,128)(2,1)S(1)} %bitcast.164), channel_id=1, source_target_pairs={{0,2},{1,3},{2,0},{3,1},{4,6},{5,7},{6,4},{7,5},{8,10},{9,11},{10,... | collective-permute-start | bytes 1179656 | tf_op jit(solution)/shard_map/ppermute | solution.py:127
  183.1 46.3 %collective-permute-start.20 = (bf16[128,1536]{1,0:T(8,128)(2,1)S(1)}, bf16[128,1536]{1,0:T(8,128)(2,1)S(1)}, u32[]{:S(2)}, u32[]{:S(2)}) collective-permute-start(bf16[128,1536]{1,0:T(8,128)(2,1)S(1)} %bitcast.165), channel_id=1, source_target_pairs={{0,3},{1,0},{2,1},{3,2},{4,7},{5,4},{6,5},{7,6},{8,11},{9,8},{10,9... | collective-permute-start | bytes 1179656 | tf_op jit(solution)/shard_map/ppermute | solution.py:127
  234.3 3.6 collective-permute-start.22
  249.6 132.9 %reduce-scatter.8.cloned.1.call-start = ((), (), s32[]{:S(2)}) async-start(), calls=%async_computation.8 | async-start | bytes 983040 | tf_op jit(solution)/shard_map/reduce_scatter | solution.py:269
  249.6 6.2 %collective-permute-start.23 = (bf16[128,3072]{1,0:T(8,128)(2,1)}, bf16[128,3072]{1,0:T(8,128)(2,1)}, u32[]{:S(2)}, u32[]{:S(2)}) collective-permute-start(bf16[128,3072]{1,0:T(8,128)(2,1)} %get-tuple-element.59), channel_id=1, source_target_pairs={{0,4},{4,0},{8,12},{12,8},{1,5},{5,1},{9,13},{13,9},{2,6},{6,2},{1... | collective-permute-start | bytes 2359304 | tf_op jit(solution)/shard_map/ppermute | solution.py:101
  254.4 19.9 %collective-permute-start.25 = (bf16[128,3072]{1,0:T(8,128)(2,1)}, bf16[128,3072]{1,0:T(8,128)(2,1)}, u32[]{:S(2)}, u32[]{:S(2)}) collective-permute-start(bf16[128,3072]{1,0:T(8,128)(2,1)} %add_convert_fusion.1), channel_id=1, source_target_pairs={{0,8},{4,12},{8,0},{12,4},{1,9},{5,13},{9,1},{13,5},{2,10},{6,14},... | collective-permute-start | bytes 2359304 | tf_op jit(solution)/shard_map/ppermute | solution.py:101
  277.4 26.6 %collective-permute-start.27 = (bf16[128,3072]{1,0:T(8,128)(2,1)}, bf16[128,3072]{1,0:T(8,128)(2,1)}, u32[]{:S(2)}, u32[]{:S(2)}) collective-permute-start(bf16[128,3072]{1,0:T(8,128)(2,1)} %fusion.33), channel_id=1, source_target_pairs={{0,8},{4,12},{8,0},{12,4},{1,9},{5,13},{9,1},{13,5},{2,10},{6,14},... | collective-permute-start | bytes 2359304 | tf_op jit(solution)/shard_map/ppermute | solution.py:101
  306.0 4.7 %collective-permute-start.26 = (bf16[128,3072]{1,0:T(8,128)(2,1)}, bf16[128,3072]{1,0:T(8,128)(2,1)S(1)}, u32[]{:S(2)}, u32[]{:S(2)}) collective-permute-start(bf16[128,3072]{1,0:T(8,128)(2,1)} %fusion.33), channel_id=1, source_target_pairs={{0,4},{4,0},{8,12},{12,8},{1,5},{5,1},{9,13},{13,9},{2,6},{6,2},{1... | collective-permute-start | bytes 2359304 | tf_op jit(solution)/shard_map/ppermute | solution.py:101
  306.5 4.2 %collective-permute-start.28 = (bf16[128,3072]{1,0:T(8,128)(2,1)}, bf16[128,3072]{1,0:T(8,128)(2,1)S(1)}, u32[]{:S(2)}, u32[]{:S(2)}) collective-permute-start(bf16[128,3072]{1,0:T(8,128)(2,1)} %collective-permute-done.27), channel_id=1, source_target_pairs={{0,4},{4,0},{8,12},{12,8},{1,5},{5,1},{9,13},{13,9},{2,6},{6,2},{1... | collective-permute-start | bytes 2359304 | tf_op jit(solution)/shard_map/ppermute | solution.py:101
  306.6 5.9 %collective-permute-start.29 = (bf16[128,3072]{1,0:T(8,128)(2,1)}, bf16[128,3072]{1,0:T(8,128)(2,1)S(1)}, u32[]{:S(2)}, u32[]{:S(2)}) collective-permute-start(bf16[128,3072]{1,0:T(8,128)(2,1)} %get-tuple-element.57), channel_id=1, source_target_pairs={{0,4},{4,0},{8,12},{12,8},{1,5},{5,1},{9,13},{13,9},{2,6},{6,2},{1... | collective-permute-start | bytes 2359304 | tf_op jit(solution)/shard_map/ppermute | solution.py:101
  309.2 19.6 %collective-permute-start.31 = (bf16[128,3072]{1,0:T(8,128)(2,1)S(1)}, bf16[128,3072]{1,0:T(8,128)(2,1)S(1)}, u32[]{:S(2)}, u32[]{:S(2)}) collective-permute-start(bf16[128,3072]{1,0:T(8,128)(2,1)S(1)} %add_convert_fusion), channel_id=1, source_target_pairs={{0,8},{4,12},{8,0},{12,4},{1,9},{5,13},{9,1},{13,5},{2,10},{6,14},... | collective-permute-start | bytes 2359304 | tf_op jit(solution)/shard_map/ppermute | solution.py:101
  329.6 18.8 %collective-permute-start.33 = (bf16[128,3072]{1,0:T(8,128)(2,1)S(1)}, bf16[128,3072]{1,0:T(8,128)(2,1)S(1)}, u32[]{:S(2)}, u32[]{:S(2)}) collective-permute-start(bf16[128,3072]{1,0:T(8,128)(2,1)S(1)} %fusion.41), channel_id=1, source_target_pairs={{0,8},{4,12},{8,0},{12,4},{1,9},{5,13},{9,1},{13,5},{2,10},{6,14},... | collective-permute-start | bytes 2359304 | tf_op jit(solution)/shard_map/ppermute | solution.py:101
  340.1 8.9 %collective-permute-start.32 = (bf16[128,3072]{1,0:T(8,128)(2,1)S(1)}, bf16[128,3072]{1,0:T(8,128)(2,1)S(1)}, u32[]{:S(2)}, u32[]{:S(2)}) collective-permute-start(bf16[128,3072]{1,0:T(8,128)(2,1)S(1)} %fusion.41), channel_id=1, source_target_pairs={{0,4},{4,0},{8,12},{12,8},{1,5},{5,1},{9,13},{13,9},{2,6},{6,2},{1... | collective-permute-start | bytes 2359304 | tf_op jit(solution)/shard_map/ppermute | solution.py:101
  (27 other events, 342.1 us)
Sparse Core Ops, SparseCore 0:
  12.4 39.7 all-gather.5
  54.4 36.0 all-gather.3
  135.7 33.4 reduce-scatter.3
  172.1 58.5 reduce-scatter.5
  249.7 45.9 all-gather.7
  358.0 24.4 reduce-scatter.7
where the time goes:
time: 396 us; the launch traced here: 391 us
  waiting for transfers between devices  208 us (53%)
  matrix products  56.3 us (14%)
  local copies, waits for them, and re-layouts  46.1 us (12%)
  other arithmetic  41.6 us (11%)
  starting transfers between devices  25.3 us (6%)
  between operations  14.2 us (4%)
    ppermute x32, waiting for transfers between devices, swap_row(): return lax.ppermute(value, 'row', [(r, r ^ distance) for r in range(size)])  103 us
    ppermute x3, waiting for transfers between devices, shift_col(): lax.ppermute(value, 'col', [(c, (c + distance) % size) for c in range(siz...  44.1 us
    reduce_scatter x1, waiting for transfers between devices, head_layer(): mlp = lax.psum_scatter(total, 'col', scatter_dimension=0, tiled=True)  24.6 us
    ppermute x32, starting transfers between devices, swap_row(): return lax.ppermute(value, 'row', [(r, r ^ distance) for r in range(size)])  20.8 us
    all_gather x2, waiting for transfers between devices, head_layer(): gathered = [lax.all_gather(x, 'col', axis=0, tiled=True) for x in x_parts]  19.3 us
    dot_general x2, matrix products, project(): jnp.dot(first, w_flat, preferred_element_type=jnp.float32).astype(BF)  18.8 us
    all_gather x1, waiting for transfers between devices, residual(): return (mixed, lax.all_gather(second, 'col', axis=0, tiled=True))  16.8 us
    unnamed x39, local copies, waits for them, and re-layouts  16.8 us
  transfers between devices with their start and end apart: 41, of which 26 were waited for; matrix products, arithmetic and copies ran while one was open for 27% of the time, Pallas kernels for 0%

commit v1 on v0

--- a/solution.py
+++ b/solution.py
@@ -2,10 +2,36 @@
 import jax.numpy as jnp
 from jax import lax
 from jax.sharding import PartitionSpec as P
+from jax.lax import axis_index, axis_size, ppermute
 
 D = 6144
 HEAD_DIM = 128
 eps = 1e-06
+
+
+def post_tails(row_data, dim_k):
+    s_next = list(row_data.shape[1:])
+    s_next[dim_k] *= row_data.shape[0]
+    return jnp.moveaxis(row_data, 0, dim_k).reshape(s_next)
+
+
+def _derive_panels(raw, shard_axis):
+    p_count = axis_size(shard_axis)
+    oldest = raw[None]
+    for tick in range(p_count.bit_length() - 1):
+        v_now = 1 << tick
+        row_out = ppermute(
+            oldest, axis_name=shard_axis, perm=[(nth, nth ^ v_now) for nth in range(p_count)]
+        )
+        small = jnp.stack([oldest, row_out])
+        carry_in = axis_index(shard_axis)
+        main = carry_in >> tick & 1
+        oldest = jnp.where(main == 0, small, small[::-1]).reshape(-1, *raw.shape)
+    return oldest
+
+
+def lay_the_circles(point, local_array, dim_i):
+    return post_tails(_derive_panels(point, local_array), dim_i)
 
 
 def normalize(values, shift, scale):
@@ -225,7 +251,7 @@
             seconds[-1], second = lax.optimization_barrier((seconds[-1], second))
         if g < GROUPS - 1:
             return (mixed, gather_col(second).reshape(tokens, feat_rows))
-        return (mixed, lax.all_gather(second, "col", axis=0, tiled=True))
+        return (mixed, lay_the_circles(second, "col", 0))
 
     def expand(g, second_all):
         partial = jnp.dot(second_all, w_up, preferred_element_type=jnp.float32).astype(BF)

time: 396 us -> 411 us (1.038)
  starting transfers between devices: 25.3 us -> 36.8 us
    ppermute x0 -> x2, waiting for transfers between devices: none -> 32.1 us  [_derive_panels(): ppermute(oldest, axis_name=shard_axis, perm=[(nth, nth ^ v_now) for nth i...]
    all_gather x1 -> x0, waiting for transfers between devices: 16.8 us -> none  [residual(): return (mixed, lax.all_gather(second, 'col', axis=0, tiled=True))]
    ppermute x0 -> x2, starting transfers between devices: none -> 11.8 us  [_derive_panels(): ppermute(oldest, axis_name=shard_axis, perm=[(nth, nth ^ v_now) for nth i...]
    ppermute x32, waiting for transfers between devices: 103 us -> 93.4 us  [swap_row(): return lax.ppermute(value, 'row', [(r, r ^ distance) for r in range(size)])]
    unnamed x39 -> x51, local copies, waits for them, and re-layouts: 16.8 us -> 18.9 us
  transfers between devices with their start and end apart: 41 -> 42, of which waited for: 26 -> 27; matrix products, arithmetic and copies ran while one was open for 27% -> 27% of each run, Pallas kernels for 0% -> 0%
where the time goes in v1:
time: 411 us; the launch traced here: 407 us
  waiting for transfers between devices  211 us (51%)
  matrix products  57.2 us (14%)
  local copies, waits for them, and re-layouts  48.4 us (12%)
  other arithmetic  39.1 us (10%)
  starting transfers between devices  36.8 us (9%)
  between operations  14 us (3%)
    ppermute x32, waiting for transfers between devices, swap_row(): return lax.ppermute(value, 'row', [(r, r ^ distance) for r in range(size)])  93.4 us
    ppermute x3, waiting for transfers between devices, shift_col(): lax.ppermute(value, 'col', [(c, (c + distance) % size) for c in range(siz...  44.1 us
    ppermute x2, waiting for transfers between devices, _derive_panels(): ppermute(oldest, axis_name=shard_axis, perm=[(nth, nth ^ v_now) for nth i...  32.1 us
    reduce_scatter x1, waiting for transfers between devices, head_layer(): mlp = lax.psum_scatter(total, 'col', scatter_dimension=0, tiled=True)  22.1 us
    ppermute x32, starting transfers between devices, swap_row(): return lax.ppermute(value, 'row', [(r, r ^ distance) for r in range(size)])  20.6 us
    all_gather x2, waiting for transfers between devices, head_layer(): gathered = [lax.all_gather(x, 'col', axis=0, tiled=True) for x in x_parts]  19.3 us
    unnamed x51, local copies, waits for them, and re-layouts  18.9 us
    dot_general x2, matrix products, project(): jnp.dot(first, w_flat, preferred_element_type=jnp.float32).astype(BF)  18.8 us
  transfers between devices with their start and end apart: 42, of which 27 were waited for; matrix products, arithmetic and copies ran while one was open for 27% of the time, Pallas kernels for 0%

profile of v1, /device:TPU:0, one launch (start us, length us, event | category | flops | bytes accessed | tf_op | source)
XLA Modules:
  0.0 406.7 jit_solution(15372540942541372390)
XLA Ops:
  6.5 2.5 reshape.360
  12.3 12.7 %copy.32 = bf16[1536,3,1024]{0,2,1:T(8,128)(2,1)} copy(bf16[1536,3,1024]{2,0,1:T(8,128)(2,1)} %param.10) | data formatting | bytes 18874368 | tf_op args[2]
  24.9 7.9 %copy.33 = bf16[1536,4,3,256]{0,3,2,1:T(8,128)(2,1)} copy(bf16[1536,4,3,256]{0,3,1,2:T(8,128)(2,1)} %bitcast.155) | data formatting | bytes 18874368 | tf_op jit(solution)/shard_map/transpose | solution.py:214
  32.9 19.3 %all-gather.5.cloned.1.call-done = bf16[512,1536]{1,0:T(8,128)(2,1)} async-done(((bf16[128,1536]{1,0:T(8,128)(2,1)}), bf16[512,1536]{1,0:T(8,128)(2,1)}) %all-gather.5.cloned.1.call-update) | async-done | bytes 1572880 | tf_op jit(solution)/shard_map/all_gather | solution.py:221
  59.1 2.7 fusion.4
  61.8 9.6 %convolution_convert_fusion.3 = bf16[512,3072]{1,0:T(8,128)(2,1)S(1)} fusion(bf16[512,1536]{1,0:T(8,128)(2,1)S(1)} %fusion.4, bf16[1536,3072]{0,1:T(8,128)(2,1)} %bitcast.161), kind=kOutput, calls=%fused_computation.9 | convolution fusion | flops 4833411072 | bytes 14155776 | tf_op jit(solution)/shard_map/dot_general | solution.py:229
  76.2 2.5 add_convert_fusion.5
  80.2 18.4 %collective-permute-done.4 = bf16[512,768]{1,0:T(8,128)(2,1)} collective-permute-done((bf16[512,768]{1,0:T(8,128)(2,1)}, bf16[512,768]{1,0:T(8,128)(2,1)}, u32[]{:S(2)}, u32[]{:S(2)}) %collective-permute-start.4) | collective-permute-done | bytes 786464 | tf_op jit(solution)/shard_map/ppermute | solution.py:127
  98.6 2.8 add_convert_fusion.4
  101.4 2.7 reshape.365
  112.8 9.1 %convolution_convert_fusion.2 = bf16[512,3072]{1,0:T(8,128)(2,1)S(1)} fusion(bf16[512,1536]{1,0:T(8,128)(2,1)S(1)} %fusion.9, bf16[1536,3072]{0,1:T(8,128)(2,1)} %bitcast.162), kind=kOutput, calls=%fused_computation.8 | convolution fusion | flops 4833411072 | bytes 14155776 | tf_op jit(solution)/shard_map/dot_general | solution.py:229
  128.7 2.4 add_convert_fusion.3
  132.6 3.0 convolution_convert_fusion.5
  135.6 15.4 %collective-permute-done.12 = bf16[512,768]{1,0:T(8,128)(2,1)} collective-permute-done((bf16[512,768]{1,0:T(8,128)(2,1)}, bf16[512,768]{1,0:T(8,128)(2,1)}, u32[]{:S(2)}, u32[]{:S(2)}) %collective-permute-start.12) | collective-permute-done | bytes 786464 | tf_op jit(solution)/shard_map/ppermute | solution.py:127
  151.0 2.8 add_convert_fusion.2
  153.8 2.9 reshape.370
  161.4 6.1 %collective-permute-done.14 = bf16[512,256]{1,0:T(8,128)(2,1)S(1)} collective-permute-done((bf16[512,256]{1,0:T(8,128)(2,1)S(1)}, bf16[512,256]{1,0:T(8,128)(2,1)S(1)}, u32[]{:S(2)}, u32[]{:S(2)}) %collective-permute-start.14) | collective-permute-done | bytes 262176 | tf_op jit(solution)/shard_map/ppermute | solution.py:127
  169.0 3.0 convolution_convert_fusion.4
  177.5 2.1 collective-permute-done.17
  183.2 2.2 collective-permute-start.20
  185.4 17.9 %collective-permute-done.18 = bf16[128,1536]{1,0:T(8,128)(2,1)S(1)} collective-permute-done((bf16[128,1536]{1,0:T(8,128)(2,1)S(1)}, bf16[128,1536]{1,0:T(8,128)(2,1)S(1)}, u32[]{:S(2)}, u32[]{:S(2)}) %collective-permute-start.18) | collective-permute-done | bytes 393248 | tf_op jit(solution)/shard_map/ppermute | solution.py:153
  203.4 26.2 %collective-permute-done.19 = bf16[128,1536]{1,0:T(8,128)(2,1)S(1)} collective-permute-done((bf16[128,1536]{1,0:T(8,128)(2,1)S(1)}, bf16[128,1536]{1,0:T(8,128)(2,1)S(1)}, u32[]{:S(2)}, u32[]{:S(2)}) %collective-permute-start.19) | collective-permute-done | bytes 393248 | tf_op jit(solution)/shard_map/ppermute | solution.py:153
  239.5 10.3 %collective-permute-start.23 = (bf16[1,128,1536]{2,1,0:T(8,128)(2,1)S(1)}, bf16[1,128,1536]{2,1,0:T(8,128)(2,1)S(1)}, u32[]{:S(2)}, u32[]{:S(2)}) collective-permute-start(bf16[1,128,1536]{2,1,0:T(8,128)(2,1)S(1)} %bitcast.181), channel_id=1, source_target_pairs={{0,1},{1,0},{2,3},{3,2},{4,5},{5,4},{6,7},{7,6},{8,9},{9,8},{10,11... | collective-permute-start | bytes 1179656 | tf_op jit(solution)/shard_map/ppermute | solution.py:23
  249.8 8.1 %convolution_convert_fusion.1 = bf16[512,3072]{1,0:T(8,128)(2,1)S(1)} fusion(bf16[512,1536]{1,0:T(8,128)(2,1)} %bitcast.171, bf16[1536,3072]{1,0:T(8,128)(2,1)} %param.12), kind=kOutput, calls=%fused_computation.7 | convolution fusion | flops 4833411072 | bytes 14155776 | tf_op jit(solution)/shard_map/dot_general | solution.py:257
  265.4 32.1 %collective-permute-done.24 = bf16[2,128,1536]{2,1,0:T(8,128)(2,1)S(1)} collective-permute-done((bf16[2,128,1536]{2,1,0:T(8,128)(2,1)S(1)}, bf16[2,128,1536]{2,1,0:T(8,128)(2,1)S(1)}, u32[]{:S(2)}, u32[]{:S(2)}) %collective-permute-start.24) | collective-permute-done | bytes 786464 | tf_op jit(solution)/shard_map/ppermute | solution.py:23
  303.9 9.1 %convolution_convert_fusion = bf16[512,3072]{1,0:T(8,128)(2,1)S(1)} fusion(bf16[512,1536]{1,0:T(8,128)(2,1)S(1)} %bitcast.178, bf16[1536,3072]{1,0:T(8,128)(2,1)} %param.12), kind=kOutput, calls=%fused_computation.6 | convolution fusion | flops 4833411072 | bytes 14155776 | tf_op jit(solution)/shard_map/dot_general | solution.py:257
  313.0 8.9 %collective-permute-done.29 = bf16[128,3072]{1,0:T(8,128)(2,1)S(1)} collective-permute-done((bf16[128,3072]{1,0:T(8,128)(2,1)S(1)}, bf16[128,3072]{1,0:T(8,128)(2,1)S(1)}, u32[]{:S(2)}, u32[]{:S(2)}) %collective-permute-start.29) | collective-permute-done | bytes 786464 | tf_op jit(solution)/shard_map/ppermute | solution.py:127
  329.2 17.7 %collective-permute-done.33 = bf16[128,3072]{1,0:T(8,128)(2,1)S(1)} collective-permute-done((bf16[128,3072]{1,0:T(8,128)(2,1)S(1)}, bf16[128,3072]{1,0:T(8,128)(2,1)S(1)}, u32[]{:S(2)}, u32[]{:S(2)}) %collective-permute-start.33) | collective-permute-done | bytes 786464 | tf_op jit(solution)/shard_map/ppermute | solution.py:127
  349.2 8.9 %fusion.10 = f32[512,1536]{1,0:T(8,128)S(1)} fusion(bf16[3072,1536]{1,0:T(8,128)(2,1)} %param.14, bf16[128,3072]{1,0:T(8,128)(2,1)S(1)} %get-tuple-element.48, bf16[128,3072]{1,0:T(8,128)(2,1)S(1)} %get-tuple-element.49, bf16[128,3072]{1,0:T(8,128)(2,1)S(1)} %get-tuple-element.50, bf16[128,3072]{1,0:T(8,128)(2,1)S(1)} %get-tuple-element.47), kind=kOutput, calls=%fused_computation.20 | convolution fusion | flops 4844421120 | bytes 15728640 | tf_op jit(solution)/shard_map/dot_general | solution.py:267
  358.2 8.3 %collective-permute-done.35 = bf16[128,3072]{1,0:T(8,128)(2,1)S(1)} collective-permute-done((bf16[128,3072]{1,0:T(8,128)(2,1)S(1)}, bf16[128,3072]{1,0:T(8,128)(2,1)S(1)}, u32[]{:S(2)}, u32[]{:S(2)}) %collective-permute-start.35) | collective-permute-done | bytes 786464 | tf_op jit(solution)/shard_map/ppermute | solution.py:127
  369.1 5.0 %fusion.18 = f32[512,1536]{1,0:T(8,128)S(1)} fusion(bf16[3072,1536]{1,0:T(8,128)(2,1)S(1)} %bitcast.217, bf16[128,3072]{1,0:T(8,128)(2,1)S(1)} %get-tuple-element.54, bf16[128,3072]{1,0:T(8,128)(2,1)S(1)} %get-tuple-element.55, bf16[128,3072]{1,0:T(8,128)(2,1)S(1)} %get-tuple-element.56, bf16[128,3072]{1,0:T(8,128)(2,1)S(1)} %get-tuple-element.53), kind=kOutput, calls=%fused_computation.28 | convolution fusion | flops 4844421120 | bytes 15728640 | tf_op jit(solution)/shard_map/dot_general | solution.py:267
  375.9 22.1 %reduce-scatter.8.cloned.1.call-done = bf16[64,1536]{1,0:T(8,128)(2,1)} async-done(((bf16[256,1536]{1,0:T(8,128)(2,1)}), bf16[64,1536]{1,0:T(8,128)(2,1)}) %reduce-scatter.8.cloned.1.call-update) | async-done | bytes 196624 | tf_op jit(solution)/shard_map/reduce_scatter | solution.py:295
  (207 shorter events, 87.8 us)
Async XLA Ops:
  6.5 45.6 %all-gather.5.cloned.1.call-start = ((), (), s32[]{:S(2)}) async-start(), calls=%async_computation.4 | async-start | bytes 1966080 | tf_op jit(solution)/shard_map/all_gather | solution.py:221
  12.2 89.2 %all-gather.3.cloned.1.call-start = ((), (), s32[]{:S(2)}) async-start(), calls=%async_computation.3 | async-start | bytes 1966080 | tf_op jit(solution)/shard_map/all_gather | solution.py:221
  54.3 118.5 %reduce-scatter.4.cloned.1.call-start = ((), (), s32[]{:S(2)}) async-start(), calls=%async_computation.5 | async-start | bytes 1966080 | tf_op jit(solution)/shard_map/reduce_scatter | solution.py:240
  55.4 3.7 collective-permute-start.1
  73.6 6.6 %collective-permute-start.2 = (bf16[512,768]{1,0:T(8,128)(2,1)}, bf16[512,768]{1,0:T(8,128)(2,1)}, u32[]{:S(2)}, u32[]{:S(2)}) collective-permute-start(bf16[512,768]{1,0:T(8,128)(2,1)} %get-tuple-element.63), channel_id=1, source_target_pairs={{0,4},{4,0},{8,12},{12,8},{1,5},{5,1},{9,13},{13,9},{2,6},{6,2},{1... | collective-permute-start | bytes 2359304 | tf_op jit(solution)/shard_map/ppermute | solution.py:127
  78.7 19.9 %collective-permute-start.4 = (bf16[512,768]{1,0:T(8,128)(2,1)}, bf16[512,768]{1,0:T(8,128)(2,1)}, u32[]{:S(2)}, u32[]{:S(2)}) collective-permute-start(bf16[512,768]{1,0:T(8,128)(2,1)} %add_convert_fusion.5), channel_id=1, source_target_pairs={{0,8},{4,12},{8,0},{12,4},{1,9},{5,13},{9,1},{13,5},{2,10},{6,14},... | collective-permute-start | bytes 2359304 | tf_op jit(solution)/shard_map/ppermute | solution.py:127
  107.9 3.7 collective-permute-start.9
  110.8 13.8 %collective-permute-start.6 = (bf16[512,256]{1,0:T(8,128)(2,1)}, bf16[512,256]{1,0:T(8,128)(2,1)}, u32[]{:S(2)}, u32[]{:S(2)}) collective-permute-start(bf16[512,256]{1,0:T(8,128)(2,1)} %bitcast.154), channel_id=1, source_target_pairs={{0,8},{4,12},{8,0},{12,4},{1,9},{5,13},{9,1},{13,5},{2,10},{6,14},... | collective-permute-start | bytes 786440 | tf_op jit(solution)/shard_map/ppermute | solution.py:127
  124.1 4.6 %collective-permute-start.11 = (bf16[512,768]{1,0:T(8,128)(2,1)}, bf16[512,768]{1,0:T(8,128)(2,1)}, u32[]{:S(2)}, u32[]{:S(2)}) collective-permute-start(bf16[512,768]{1,0:T(8,128)(2,1)} %get-tuple-element.62), channel_id=1, source_target_pairs={{0,4},{4,0},{8,12},{12,8},{1,5},{5,1},{9,13},{13,9},{2,6},{6,2},{1... | collective-permute-start | bytes 2359304 | tf_op jit(solution)/shard_map/ppermute | solution.py:127
  124.1 3.0 collective-permute-start.5
  124.6 11.0 %collective-permute-start.10 = (bf16[512,768]{1,0:T(8,128)(2,1)}, bf16[512,768]{1,0:T(8,128)(2,1)}, u32[]{:S(2)}, u32[]{:S(2)}) collective-permute-start(bf16[512,768]{1,0:T(8,128)(2,1)} %get-tuple-element.61), channel_id=1, source_target_pairs={{0,4},{4,0},{8,12},{12,8},{1,5},{5,1},{9,13},{13,9},{2,6},{6,2},{1... | collective-permute-start | bytes 2359304 | tf_op jit(solution)/shard_map/ppermute | solution.py:127
  131.1 19.9 %collective-permute-start.12 = (bf16[512,768]{1,0:T(8,128)(2,1)}, bf16[512,768]{1,0:T(8,128)(2,1)}, u32[]{:S(2)}, u32[]{:S(2)}) collective-permute-start(bf16[512,768]{1,0:T(8,128)(2,1)} %add_convert_fusion.3), channel_id=1, source_target_pairs={{0,8},{4,12},{8,0},{12,4},{1,9},{5,13},{9,1},{13,5},{2,10},{6,14},... | collective-permute-start | bytes 2359304 | tf_op jit(solution)/shard_map/ppermute | solution.py:127
  135.6 95.3 %reduce-scatter.6.cloned.1.call-start = ((), (), s32[]{:S(2)}) async-start(), calls=%async_computation.6 | async-start | bytes 1966080 | tf_op jit(solution)/shard_map/reduce_scatter | solution.py:240
  159.8 7.6 %collective-permute-start.14 = (bf16[512,256]{1,0:T(8,128)(2,1)S(1)}, bf16[512,256]{1,0:T(8,128)(2,1)S(1)}, u32[]{:S(2)}, u32[]{:S(2)}) collective-permute-start(bf16[512,256]{1,0:T(8,128)(2,1)S(1)} %bitcast.192), channel_id=1, source_target_pairs={{0,8},{4,12},{8,0},{12,4},{1,9},{5,13},{9,1},{13,5},{2,10},{6,14},... | collective-permute-start | bytes 786440 | tf_op jit(solution)/shard_map/ppermute | solution.py:127
  161.3 6.1 %collective-permute-start.13 = (bf16[512,256]{1,0:T(8,128)(2,1)S(1)}, bf16[512,256]{1,0:T(8,128)(2,1)S(1)}, u32[]{:S(2)}, u32[]{:S(2)}) collective-permute-start(bf16[512,256]{1,0:T(8,128)(2,1)S(1)} %bitcast.193), channel_id=1, source_target_pairs={{0,4},{4,0},{8,12},{12,8},{1,5},{5,1},{9,13},{13,9},{2,6},{6,2},{1... | collective-permute-start | bytes 786440 | tf_op jit(solution)/shard_map/ppermute | solution.py:127
  172.1 226.0 %reduce-scatter.8.cloned.1.call-start = ((), (), s32[]{:S(2)}) async-start(), calls=%async_computation.7 | async-start | bytes 983040 | tf_op jit(solution)/shard_map/reduce_scatter | solution.py:295
  175.9 3.7 collective-permute-start.17
  181.1 22.2 %collective-permute-start.18 = (bf16[128,1536]{1,0:T(8,128)(2,1)S(1)}, bf16[128,1536]{1,0:T(8,128)(2,1)S(1)}, u32[]{:S(2)}, u32[]{:S(2)}) collective-permute-start(bf16[128,1536]{1,0:T(8,128)(2,1)S(1)} %bitcast.172), channel_id=1, source_target_pairs={{0,1},{1,2},{2,3},{3,0},{4,5},{5,6},{6,7},{7,4},{8,9},{9,10},{10,1... | collective-permute-start | bytes 1179656 | tf_op jit(solution)/shard_map/ppermute | solution.py:153
  181.7 47.8 %collective-permute-start.19 = (bf16[128,1536]{1,0:T(8,128)(2,1)S(1)}, bf16[128,1536]{1,0:T(8,128)(2,1)S(1)}, u32[]{:S(2)}, u32[]{:S(2)}) collective-permute-start(bf16[128,1536]{1,0:T(8,128)(2,1)S(1)} %bitcast.173), channel_id=1, source_target_pairs={{0,2},{1,3},{2,0},{3,1},{4,6},{5,7},{6,4},{7,5},{8,10},{9,11},{10,... | collective-permute-start | bytes 1179656 | tf_op jit(solution)/shard_map/ppermute | solution.py:153
  183.2 46.3 %collective-permute-start.20 = (bf16[128,1536]{1,0:T(8,128)(2,1)S(1)}, bf16[128,1536]{1,0:T(8,128)(2,1)S(1)}, u32[]{:S(2)}, u32[]{:S(2)}) collective-permute-start(bf16[128,1536]{1,0:T(8,128)(2,1)S(1)} %bitcast.174), channel_id=1, source_target_pairs={{0,3},{1,0},{2,1},{3,2},{4,7},{5,4},{6,5},{7,6},{8,11},{9,8},{10,9... | collective-permute-start | bytes 1179656 | tf_op jit(solution)/shard_map/ppermute | solution.py:153
  234.4 3.6 collective-permute-start.22
  239.5 20.5 %collective-permute-start.23 = (bf16[1,128,1536]{2,1,0:T(8,128)(2,1)S(1)}, bf16[1,128,1536]{2,1,0:T(8,128)(2,1)S(1)}, u32[]{:S(2)}, u32[]{:S(2)}) collective-permute-start(bf16[1,128,1536]{2,1,0:T(8,128)(2,1)S(1)} %bitcast.181), channel_id=1, source_target_pairs={{0,1},{1,0},{2,3},{3,2},{4,5},{5,4},{6,7},{7,6},{8,9},{9,8},{10,11... | collective-permute-start | bytes 1179656 | tf_op jit(solution)/shard_map/ppermute | solution.py:23
  260.3 37.2 %collective-permute-start.24 = (bf16[2,128,1536]{2,1,0:T(8,128)(2,1)S(1)}, bf16[2,128,1536]{2,1,0:T(8,128)(2,1)S(1)}, u32[]{:S(2)}, u32[]{:S(2)}) collective-permute-start(bf16[2,128,1536]{2,1,0:T(8,128)(2,1)S(1)} %get-tuple-element.78), channel_id=1, source_target_pairs={{0,2},{1,3},{2,0},{3,1},{4,6},{5,7},{6,4},{7,5},{8,10},{9,11},{10,... | collective-permute-start | bytes 2359304 | tf_op jit(solution)/shard_map/ppermute | solution.py:23
  261.8 38.2 %collective-permute-start.25 = (bf16[128,3072]{1,0:T(8,128)(2,1)}, bf16[128,3072]{1,0:T(8,128)(2,1)S(1)}, u32[]{:S(2)}, u32[]{:S(2)}) collective-permute-start(bf16[128,3072]{1,0:T(8,128)(2,1)} %get-tuple-element.59), channel_id=1, source_target_pairs={{0,4},{4,0},{8,12},{12,8},{1,5},{5,1},{9,13},{13,9},{2,6},{6,2},{1... | collective-permute-start | bytes 2359304 | tf_op jit(solution)/shard_map/ppermute | solution.py:127
  263.8 36.1 %collective-permute-start.27 = (bf16[128,3072]{1,0:T(8,128)(2,1)S(1)}, bf16[128,3072]{1,0:T(8,128)(2,1)S(1)}, u32[]{:S(2)}, u32[]{:S(2)}) collective-permute-start(bf16[128,3072]{1,0:T(8,128)(2,1)S(1)} %add_convert_fusion.1), channel_id=1, source_target_pairs={{0,8},{4,12},{8,0},{12,4},{1,9},{5,13},{9,1},{13,5},{2,10},{6,14},... | collective-permute-start | bytes 2359304 | tf_op jit(solution)/shard_map/ppermute | solution.py:127
  302.3 19.6 %collective-permute-start.29 = (bf16[128,3072]{1,0:T(8,128)(2,1)S(1)}, bf16[128,3072]{1,0:T(8,128)(2,1)S(1)}, u32[]{:S(2)}, u32[]{:S(2)}) collective-permute-start(bf16[128,3072]{1,0:T(8,128)(2,1)S(1)} %fusion.33), channel_id=1, source_target_pairs={{0,8},{4,12},{8,0},{12,4},{1,9},{5,13},{9,1},{13,5},{2,10},{6,14},... | collective-permute-start | bytes 2359304 | tf_op jit(solution)/shard_map/ppermute | solution.py:127
  324.2 4.6 %collective-permute-start.28 = (bf16[128,3072]{1,0:T(8,128)(2,1)}, bf16[128,3072]{1,0:T(8,128)(2,1)S(1)}, u32[]{:S(2)}, u32[]{:S(2)}) collective-permute-start(bf16[128,3072]{1,0:T(8,128)(2,1)} %copy-done.8), channel_id=1, source_target_pairs={{0,4},{4,0},{8,12},{12,8},{1,5},{5,1},{9,13},{13,9},{2,6},{6,2},{1... | collective-permute-start | bytes 2359304 | tf_op jit(solution)/shard_map/ppermute | solution.py:127
  324.7 4.1 collective-permute-start.30
  324.8 4.3 %collective-permute-start.31 = (bf16[128,3072]{1,0:T(8,128)(2,1)}, bf16[128,3072]{1,0:T(8,128)(2,1)S(1)}, u32[]{:S(2)}, u32[]{:S(2)}) collective-permute-start(bf16[128,3072]{1,0:T(8,128)(2,1)} %get-tuple-element.57), channel_id=1, source_target_pairs={{0,4},{4,0},{8,12},{12,8},{1,5},{5,1},{9,13},{13,9},{2,6},{6,2},{1... | collective-permute-start | bytes 2359304 | tf_op jit(solution)/shard_map/ppermute | solution.py:127
  327.3 19.6 %collective-permute-start.33 = (bf16[128,3072]{1,0:T(8,128)(2,1)S(1)}, bf16[128,3072]{1,0:T(8,128)(2,1)S(1)}, u32[]{:S(2)}, u32[]{:S(2)}) collective-permute-start(bf16[128,3072]{1,0:T(8,128)(2,1)S(1)} %add_convert_fusion), channel_id=1, source_target_pairs={{0,8},{4,12},{8,0},{12,4},{1,9},{5,13},{9,1},{13,5},{2,10},{6,14},... | collective-permute-start | bytes 2359304 | tf_op jit(solution)/shard_map/ppermute | solution.py:127
  347.7 18.8 %collective-permute-start.35 = (bf16[128,3072]{1,0:T(8,128)(2,1)S(1)}, bf16[128,3072]{1,0:T(8,128)(2,1)S(1)}, u32[]{:S(2)}, u32[]{:S(2)}) collective-permute-start(bf16[128,3072]{1,0:T(8,128)(2,1)S(1)} %fusion.41), channel_id=1, source_target_pairs={{0,8},{4,12},{8,0},{12,4},{1,9},{5,13},{9,1},{13,5},{2,10},{6,14},... | collective-permute-start | bytes 2359304 | tf_op jit(solution)/shard_map/ppermute | solution.py:127
  358.1 8.9 %collective-permute-start.34 = (bf16[128,3072]{1,0:T(8,128)(2,1)S(1)}, bf16[128,3072]{1,0:T(8,128)(2,1)S(1)}, u32[]{:S(2)}, u32[]{:S(2)}) collective-permute-start(bf16[128,3072]{1,0:T(8,128)(2,1)S(1)} %fusion.41), channel_id=1, source_target_pairs={{0,4},{4,0},{8,12},{12,8},{1,5},{5,1},{9,13},{13,9},{2,6},{6,2},{1... | collective-permute-start | bytes 2359304 | tf_op jit(solution)/shard_map/ppermute | solution.py:127
  (34 other events, 344.5 us)
Sparse Core Ops, SparseCore 0:
  12.3 39.7 all-gather.4
  54.4 36.0 all-gather.2
  135.7 33.4 reduce-scatter.3
  172.2 58.6 reduce-scatter.5
  376.1 21.9 reduce-scatter.7
